TPU v7x, 32 devices: a whole 2x2x4 slice. The times are simulated.
32 devices in a mesh: seq: 8 (over y, x, core), cb: 4 (over z).
Axes of the slice: x: 2, y: 2, z: 4, core: 2. Of those that a mesh axis runs over, the one named last changes fastest.
Arguments:
- hidden: bfloat16 [2, 1024, 4096], P(None, 'seq'), may hold values from -6 to 6
- temporal_gain: float32 [4096], replicated, may hold values from 0.5 to 2
- temporal_qkv: bfloat16 [3, 4096, 2048], P(None, None, 'cb'), may hold values from -10 to 10
- temporal_out: bfloat16 [2048, 4096], P('cb'), may hold values from -0.125 to 0.125
- codebook_ids: int32 [2, 1024, 4], P(None, 'seq', 'cb'), may hold values from 0 to 2047
- embedding: bfloat16 [4, 2048, 1024], P('cb'), may hold values from -6 to 6
- input_weight: bfloat16 [4, 4096, 1024], P('cb', 'seq'), may hold values from -0.09375 to 0.09375
- depth_gain: float32 [4, 1024], P('cb'), may hold values from 0.5 to 2
- depth_qkv: bfloat16 [4, 3, 1024, 1024], P('cb'), may hold values from -10 to 10
- depth_out: bfloat16 [4, 1024, 1024], P('cb'), may hold values from -0.1875 to 0.1875
Outputs:
- temporal: bfloat16 [2, 1024, 4096], P(None, 'seq')
- depth: bfloat16 [2, 1024, 4, 1024], P(None, 'seq', 'cb')
All inputs are finite; a program needn't handle non-finite values.
Results may differ from a plain program's by a relative error of at most 0.017.
Values may be sent and summed in bfloat16 or wider, within the bound.
No kernel may reach another device: no remote copies, remote signals or barrier semaphores. Data moves between devices by JAX's collectives and lax.ppermute only.
A program may use at most 128 MiB of HBM per device.

v0:
```python
import jax
import jax.numpy as jnp
from jax import lax
from jax.sharding import PartitionSpec as P

HD = 128
DW = 1024
DH = 16
DHD = 64


def normalize(values, scale):
    mean_sq = jnp.mean(values * values, axis=-1, keepdims=True)
    return values * lax.rsqrt(mean_sq + 1e-05) * scale


def shards(
    hidden,
    temporal_gain,
    temporal_qkv,
    temporal_out,
    codebook_ids,
    embedding,
    input_weight,
    depth_gain,
    depth_qkv,
    depth_out,
):
    seq_count, frames, width = hidden.shape
    head_cols = temporal_qkv.shape[2]
    head_count = head_cols // HD
    row_count = seq_count * frames
    hidden_f = hidden.astype(jnp.float32)
    normed = normalize(hidden_f, temporal_gain).astype(jnp.bfloat16).reshape(row_count, width)
    projected = []
    for which in range(3):
        part_rows = jnp.dot(normed, temporal_qkv[which], preferred_element_type=jnp.float32).astype(
            jnp.bfloat16
        )
        projected.append(part_rows.reshape(seq_count, frames, head_count, HD))
    queries = projected[0]
    query_pos = lax.axis_index("seq") * frames + jnp.arange(frames, dtype=jnp.int32)
    temporal_scale = 1.0 / jnp.sqrt(jnp.float32(HD))
    highest = jnp.full((seq_count, head_count, frames), -1e30, jnp.float32)
    key_piece = lax.all_gather(projected[1], "seq", axis=1, tiled=True)
    value_piece = lax.all_gather(projected[2], "seq", axis=1, tiled=True)
    count = key_piece.shape[1]
    scores = (
        jnp.einsum("sqhd,skhd->shqk", queries, key_piece, preferred_element_type=jnp.float32)
        * temporal_scale
    )
    key_pos = jnp.arange(count, dtype=jnp.int32)
    allowed = (key_pos[None, :] <= query_pos[:, None])[None, None]
    scores = jnp.where(allowed, scores, -1e30)
    new_high = jnp.maximum(highest, jnp.max(scores, axis=-1))
    weights = jnp.where(allowed, jnp.exp(scores - new_high[..., None]), 0.0)
    totals = jnp.sum(weights, axis=-1)
    update = jnp.einsum(
        "shqk,skhd->sqhd",
        weights.astype(jnp.bfloat16),
        value_piece,
        preferred_element_type=jnp.float32,
    )
    gathered = update
    highest, totals, gathered = (new_high, totals, gathered)
    mixed = (
        (gathered / totals.transpose(0, 2, 1)[..., None])
        .astype(jnp.bfloat16)
        .reshape(row_count, head_cols)
    )
    term = jnp.dot(mixed, temporal_out, preferred_element_type=jnp.float32)
    summed = lax.psum(term.astype(jnp.bfloat16), "cb").astype(jnp.float32)
    temporal = (hidden_f.reshape(row_count, width) + summed).astype(jnp.bfloat16)
    projected_in = jnp.dot(
        temporal,
        lax.all_gather(input_weight, "seq", axis=1, tiled=True)[0],
        preferred_element_type=jnp.float32,
    )
    entry = jnp.take(embedding[0], codebook_ids.reshape(row_count), axis=0).astype(jnp.float32)
    stream = (projected_in + entry).astype(jnp.bfloat16)
    depth_normed = normalize(stream.astype(jnp.float32), depth_gain[0]).astype(jnp.bfloat16)
    book_query = jnp.dot(depth_normed, depth_qkv[0, 0], preferred_element_type=jnp.float32).astype(
        jnp.bfloat16
    )
    book_key = jnp.dot(depth_normed, depth_qkv[0, 1], preferred_element_type=jnp.float32).astype(
        jnp.bfloat16
    )
    book_value = jnp.dot(depth_normed, depth_qkv[0, 2], preferred_element_type=jnp.float32).astype(
        jnp.bfloat16
    )
    depth_scale = 1.0 / jnp.sqrt(jnp.float32(DHD))
    books = lax.axis_size("cb")
    block_rows = row_count // books
    packed = jnp.concatenate([book_query, book_key, book_value], axis=1).reshape(
        1, books, block_rows, 3 * DW
    )
    arrived = lax.all_to_all(packed, "cb", split_axis=1, concat_axis=0, tiled=True)
    item_count = arrived.shape[2]
    body_rows = arrived.reshape(books, item_count, 3, DH, DHD)
    query_part = body_rows[:, :, 0]
    key_part = body_rows[:, :, 1]
    value_part = body_rows[:, :, 2]
    scores = (
        jnp.einsum("crhd,jrhd->crhj", query_part, key_part, preferred_element_type=jnp.float32)
        * depth_scale
    )
    numbers = jnp.arange(books, dtype=jnp.int32)
    permitted = (numbers[None, :] <= numbers[:, None])[:, None, None, :]
    scores = jnp.where(permitted, scores, -1e30)
    highest_l = jnp.max(scores, axis=-1, keepdims=True)
    weights = jnp.where(permitted, jnp.exp(scores - highest_l), 0.0)
    totals_l = jnp.sum(weights, axis=-1)[..., None]
    result = (
        jnp.einsum(
            "crhj,jrhd->crhd",
            weights.astype(jnp.bfloat16),
            value_part,
            preferred_element_type=jnp.float32,
        )
        / totals_l
    )
    result = result.astype(jnp.bfloat16).reshape(books, 1, item_count, DW)
    returned = lax.all_to_all(result, "cb", split_axis=0, concat_axis=1, tiled=True)
    book_mixed = returned.reshape(row_count, DW)
    depth = (
        jnp.dot(book_mixed, depth_out[0], preferred_element_type=jnp.float32)
        + stream.astype(jnp.float32)
    ).astype(jnp.bfloat16)
    return (temporal.reshape(seq_count, frames, width), depth.reshape(seq_count, frames, 1, DW))


def solution(mesh):
    placed = (
        P(None, "seq", None),
        P(),
        P(None, None, "cb"),
        P("cb", None),
        P(None, "seq", "cb"),
        P("cb", None, None),
        P("cb", "seq", None),
        P("cb", None),
        P("cb", None, None, None),
        P("cb", None, None),
    )
    return jax.shard_map(
        shards,
        mesh=mesh,
        in_specs=placed,
        out_specs=(P(None, "seq", None), P(None, "seq", "cb", None)),
        check_vma=False,
    )
```

profile of v0, /device:TPU:0, one launch (start us, length us, event | category | flops | bytes accessed | tf_op | source)
XLA Modules:
  0.0 334.3 jit_solution(7204706713739142722)
XLA Ops:
  13.1 3.5 %fusion.63 = bf16[256,512]{1,0:T(8,128)(2,1)S(1)} fusion(bf16[256,4096]{1,0:T(8,128)(2,1)S(1)} %bitcast.119, bf16[3,4096,512]{2,1,0:T(8,128)(2,1)} %param.12), kind=kOutput, calls=%fused_computation.54 | convolution fusion | flops 1073872896 | bytes 6553600 | tf_op jit(solution)/shard_map/dot_general | solution.py:37
  17.5 4.1 %fusion.57 = bf16[256,512]{1,0:T(8,128)(2,1)S(1)} fusion(bf16[256,4096]{1,0:T(8,128)(2,1)} %bitcast.120, bf16[3,4096,512]{2,1,0:T(8,128)(2,1)} %param.12), kind=kOutput, calls=%fused_computation.52 | convolution fusion | flops 1073872896 | bytes 6553600 | tf_op jit(solution)/shard_map/dot_general | solution.py:37
  22.6 4.1 %fusion.60 = bf16[256,512]{1,0:T(8,128)(2,1)S(1)} fusion(bf16[256,4096]{1,0:T(8,128)(2,1)} %bitcast.121, bf16[3,4096,512]{2,1,0:T(8,128)(2,1)} %param.12), kind=kOutput, calls=%fused_computation.53 | convolution fusion | flops 1073872896 | bytes 6553600 | tf_op jit(solution)/shard_map/dot_general | solution.py:37
  26.9 21.2 %all-gather.6.cloned.1.call-done = bf16[2,1024,4,128]{3,1,2,0:T(8,128)(2,1)} async-done(((bf16[2,128,4,128]{3,1,2,0:T(8,128)(2,1)}), bf16[2,1024,4,128]{3,1,2,0:T(8,128)(2,1)}) %all-gather.6.cloned.1.call-update) | async-done | bytes 2097168 | tf_op jit(solution)/shard_map/all_gather | solution.py:45
  48.1 2.6 fusion.12
  54.0 24.7 %all-gather.4.cloned.1.call-done = bf16[2,1024,4,128]{1,3,2,0:T(8,128)(2,1)} async-done(((bf16[2,128,4,128]{1,3,2,0:T(8,128)(2,1)}), bf16[2,1024,4,128]{1,3,2,0:T(8,128)(2,1)}) %all-gather.4.cloned.1.call-update) | async-done | bytes 2097168 | tf_op jit(solution)/shard_map/all_gather | solution.py:46
  78.7 4.2 %fusion.73 = bf16[2,128,4,128]{1,3,2,0:T(8,128)(2,1)S(1)} fusion(bf16[2,1024,4,128]{1,3,2,0:T(8,128)(2,1)} %all-gather.4.cloned.1.call-done, f32[2,4,128,1024]{3,2,1,0:T(8,128)} %copy-done.1, f32[2,4,128]{2,1,0:T(4,128)S(1)} %broadcast_maximum_fusion, pred[128,1024]{1,0:T(8,128)(4,1)S(1)} %iota_compare_fusion, f32[2,128,4]{1,2,0:T(4,128)S(1)} %bitcast.126), kind=kOutput, calls=%fused_computation.63 | convolution fusion | flops 273940480 | bytes 6692864 | tf_op jit(solution)/shard_map/shqk,skhd->sqhd/dot_general | solution.py:58
  83.2 4.8 %convolution_convert_fusion = bf16[256,4096]{1,0:T(8,128)(2,1)} fusion(bf16[512,4096]{1,0:T(8,128)(2,1)} %param.13, bf16[32,8,4,128]{3,2,1,0:T(4,128)(2,1)S(1)} %bitcast.124), kind=kOutput, calls=%fused_computation.3 | convolution fusion | flops 1074790400 | bytes 6553600 | tf_op jit(solution)/shard_map/dot_general | solution.py:71
  88.6 4.3 %gather_fusion = bf16[256,1024]{1,0:T(8,128)(2,1)S(1)} fusion(bf16[2048,1024]{1,0:T(8,128)(2,1)} %bitcast.117, s32[1024]{0:T(1024)S(1)} %pad_clamp_fusion), kind=kCustom, calls=%fused_computation | custom fusion | bytes 1049600 | tf_op jit(solution)/shard_map/jit(_take)/gather | solution.py:79
  92.9 81.4 %all-reduce.2.cloned.1.call-done = bf16[256,4096]{1,0:T(8,128)(2,1)} async-done(((bf16[256,4096]{1,0:T(8,128)(2,1)}), bf16[256,4096]{1,0:T(8,128)(2,1)}) %all-reduce.2.cloned.1.call-update) | async-done | bytes 2097168 | tf_op jit(solution)/shard_map/psum | solution.py:72
  174.2 4.3 %fusion.8 = bf16[256,4096]{1,0:T(8,128)(2,1)} fusion(bf16[256,4096]{1,0:T(8,128)(2,1)} %all-reduce.2.cloned.1.call-done, bf16[2,128,4096]{2,1,0:T(8,128)(2,1)} %param.10), kind=kLoop, calls=%fused_computation.11 | loop fusion | flops 4194304 | bytes 6291456 | tf_op jit(solution)/shard_map/convert_element_type | solution.py:73
  178.6 50.7 %all-gather.8.cloned.1.call-done = bf16[1,4096,1024]{2,1,0:T(8,128)(2,1)} async-done(((bf16[1,512,1024]{2,1,0:T(8,128)(2,1)}), bf16[1,4096,1024]{2,1,0:T(8,128)(2,1)}) %all-gather.8.cloned.1.call-update) | async-done | bytes 8388624 | tf_op jit(solution)/shard_map/all_gather | solution.py:76
  229.3 6.5 %fusion.66 = (f32[256]{0:T(256)S(1)}, bf16[256,1024]{1,0:T(8,128)(2,1)S(1)}) fusion(bf16[256,1024]{1,0:T(8,128)(2,1)S(1)} %gather_fusion, pred[256]{0:T(512)(128)(4,1)S(1)} %compare_and_fusion, bf16[256,4096]{1,0:T(8,128)(2,1)} %fusion.8, bf16[1,4096,1024]{2,1,0:T(8,128)(2,1)} %all-gather.8.cloned.1.call-done), kind=kOutput, calls=%fused_computation.55 | convolution fusion | flops 2149318400 | bytes 11535616 | tf_op jit(solution)/shard_map/dot_general | solution.py:74
  235.8 2.5 fusion.45
  238.3 2.4 fusion.48
  244.3 4.6 %all-to-all-start = ((bf16[1,4,64,3072]{3,2,0,1:T(8,128)(2,1)}), bf16[1,4,64,3072]{3,2,0,1:T(8,128)(2,1)}, u32[]{:S(2)}, u32[]{:S(2)}) async-start(bf16[1,4,64,3072]{3,2,0,1:T(8,128)(2,1)} %bitcast.116), calls=%async_computation | async-start | bytes 3145728 | tf_op jit(solution)/shard_map/all_to_all | solution.py:97
  248.9 37.5 %all-to-all-done = bf16[1,4,64,3072]{3,2,0,1:T(8,128)(2,1)} async-done(((bf16[1,4,64,3072]{3,2,0,1:T(8,128)(2,1)}), bf16[1,4,64,3072]{3,2,0,1:T(8,128)(2,1)}, u32[]{:S(2)}, u32[]{:S(2)}) %all-to-all-start) | async-done | bytes 1572896 | tf_op jit(solution)/shard_map/all_to_all | solution.py:97
  286.4 4.9 %reshape.154 = bf16[4,64,3,16,64]{4,3,2,1,0:T(8,128)(2,1)} reshape(bf16[1,4,64,3072]{3,2,0,1:T(8,128)(2,1)} %all-to-all-done) | data formatting | bytes 3145728 | tf_op jit(solution)/shard_map/reshape | solution.py:99
  291.3 3.5 %fusion.89 = (bf16[4,64,1,16,64]{4,3,2,1,0:T(8,128)(2,1)}, bf16[4,64,1,16,64]{4,3,2,1,0:T(8,128)(2,1)S(1)}, bf16[4,64,1,16,64]{4,3,2,1,0:T(8,128)(2,1)S(1)}) fusion(bf16[4,64,3,16,64]{4,3,2,1,0:T(8,128)(2,1)} %reshape.154), kind=kLoop, calls=%fused_computation.86 | loop fusion | bytes 3145728 | tf_op jit(solution)/shard_map/slice | solution.py:102
  294.8 2.9 fusion.69
  297.7 2.4 copy.60
  303.2 2.9 fusion.32
  307.7 17.5 %all_to_all.8 = bf16[4,1,64,1024]{3,2,1,0:T(8,128)(2,1)S(1)} all-to-all(bf16[4,1,64,1024]{3,2,1,0:T(8,128)(2,1)} %bitcast.122), channel_id=1, replica_groups=mesh['seq'=8,'cb'=4] {'cb'}, dimensions={0} | all-to-all | bytes 1048576 | tf_op jit(solution)/shard_map/all_to_all | solution.py:123
  325.2 2.5 fusion.42
  (46 shorter events, 20.5 us)
Async XLA Ops:
  7.2 318.0 %copy-start = (bf16[1,1024,1024]{2,1,0:T(8,128)(2,1)S(1)}, bf16[1,1024,1024]{2,1,0:T(8,128)(2,1)}, u32[]{:S(2)}) copy-start(bf16[1,1024,1024]{2,1,0:T(8,128)(2,1)} %param.19) | copy-start | bytes 6291460
  7.2 41.0 %all-gather.6.cloned.1.call-start = ((), (), s32[]{:S(2)}) async-start(), calls=%async_computation.3 | async-start | bytes 2359296 | tf_op jit(solution)/shard_map/all_gather | solution.py:45
  11.8 1.3 copy-start.2
  17.5 61.2 %all-gather.4.cloned.1.call-start = ((), (), s32[]{:S(2)}) async-start(), calls=%async_computation.2 | async-start | bytes 2359296 | tf_op jit(solution)/shard_map/all_gather | solution.py:46
  22.6 151.7 %all-reduce.2.cloned.1.call-start = ((), (), s32[]{:S(2)}) async-start(), calls=%async_computation.4 | async-start | bytes 4194304 | tf_op jit(solution)/shard_map/psum | solution.py:72
  50.8 1.9 copy-start.1
  83.1 5.4 %copy-start.3 = (s32[2,128,1]{1,2,0:T(1,128)S(1)}, s32[2,128,1]{1,2,0:T(1,128)}, u32[]{:S(2)}) copy-start(s32[2,128,1]{1,2,0:T(1,128)} %param.14) | copy-start | bytes 3076
  87.9 141.4 %all-gather.8.cloned.1.call-start = ((), (), s32[]{:S(2)}) async-start(), calls=%async_computation.5 | async-start | bytes 9437184 | tf_op jit(solution)/shard_map/all_gather | solution.py:76
  178.6 57.2 %copy-start.4 = (f32[1,1024]{1,0:T(1,128)S(1)}, f32[1,1024]{1,0:T(1,128)}, u32[]{:S(2)}) copy-start(f32[1,1024]{1,0:T(1,128)} %param.17) | copy-start | bytes 12292
  235.8 4.9 %copy-start.5 = (bf16[256,1024]{1,0:T(8,128)(2,1)}, bf16[256,1024]{1,0:T(8,128)(2,1)S(1)}, u32[]{:S(2)}) copy-start(bf16[256,1024]{1,0:T(8,128)(2,1)S(1)} %get-tuple-element.20) | copy-start | bytes 1572868
  244.3 42.1 %all-to-all-start = ((bf16[1,4,64,3072]{3,2,0,1:T(8,128)(2,1)}), bf16[1,4,64,3072]{3,2,0,1:T(8,128)(2,1)}, u32[]{:S(2)}, u32[]{:S(2)}) async-start(bf16[1,4,64,3072]{3,2,0,1:T(8,128)(2,1)} %bitcast.116), calls=%async_computation | async-start | bytes 3145728 | tf_op jit(solution)/shard_map/all_to_all | solution.py:97
Sparse Core Ops, SparseCore 0:
  17.6 30.4 all-gather.5
  50.6 28.0 all-gather.3
  88.1 86.1 all-reduce.1
  176.0 53.2 all-gather.7
where the time goes:
time: 335 us; the launch traced here: 334 us
  waiting for transfers between devices  216 us (64%)
  matrix products  45.2 us (13%)
  local copies, waits for them, and re-layouts  24.8 us (7%)
  blocking collectives  17.5 us (5%)
  between operations  14 us (4%)
  other arithmetic  11.9 us (4%)
  starting transfers between devices  4.93 us (1%)
    psum x1, waiting for transfers between devices, shards(): summed = lax.psum(term.astype(jnp.bfloat16), 'cb').astype(jnp.float32)  81.4 us
    all_gather x1, waiting for transfers between devices, shards(): lax.all_gather(input_weight, 'seq', axis=1, tiled=True)[0]  50.7 us
    all_to_all x1, waiting for transfers between devices, shards(): lax.all_to_all(packed, 'cb', split_axis=1, concat_axis=0, tiled=True)  37.5 us
    all_gather x1, waiting for transfers between devices, shards(): value_piece = lax.all_gather(projected[2], 'seq', axis=1, tiled=True)  24.7 us
    all_gather x1, waiting for transfers between devices, shards(): key_piece = lax.all_gather(projected[1], 'seq', axis=1, tiled=True)  21.2 us
    all_to_all x1, blocking collectives, shards(): lax.all_to_all(result, 'cb', split_axis=0, concat_axis=1, tiled=True)  17.5 us
    dot_general x3, matrix products, shards(): jnp.dot(normed, temporal_qkv[which], preferred_element_type=jnp.float32)  11.6 us
  transfers between devices with their start and end apart: 5, of which 5 were waited for; matrix products, arithmetic and copies ran while one was open for 7% of the time, Pallas kernels for 0%

commit v1 on v0

--- a/solution.py
+++ b/solution.py
@@ -94,7 +94,9 @@
     packed = jnp.concatenate([book_query, book_key, book_value], axis=1).reshape(
         1, books, block_rows, 3 * DW
     )
-    arrived = lax.all_to_all(packed, "cb", split_axis=1, concat_axis=0, tiled=True)
+    shards_2 = jnp.split(packed, lax.axis_size("cb"), axis=1)
+    received = lax.all_to_all(jnp.stack(shards_2), "cb", 0, 0)
+    arrived = jnp.concatenate(received, axis=0)
     item_count = arrived.shape[2]
     body_rows = arrived.reshape(books, item_count, 3, DH, DHD)
     query_part = body_rows[:, :, 0]

time: 335 us -> 334 us (level)
    another operation x0 -> x2, local copies, waits for them, and re-layouts: none -> 4.97 us  [the longest x1 4.87 us: shards(): body_rows = arrived.reshape(books, item_count, 3, DH, DHD)]
    reshape x1 -> x0, local copies, waits for them, and re-layouts: 4.87 us -> none  [shards(): body_rows = arrived.reshape(books, item_count, 3, DH, DHD)]
where the time goes in v1:
time: 334 us
  waiting for transfers between devices  216 us (65%)
  matrix products  45.2 us (14%)
  local copies, waits for them, and re-layouts  25 us (7%)
  blocking collectives  17.5 us (5%)
  between operations  14 us (4%)
  other arithmetic  11.1 us (3%)
  starting transfers between devices  4.96 us (1%)
    psum x1, waiting for transfers between devices, shards(): summed = lax.psum(term.astype(jnp.bfloat16), 'cb').astype(jnp.float32)  81.3 us
    all_gather x1, waiting for transfers between devices, shards(): lax.all_gather(input_weight, 'seq', axis=1, tiled=True)[0]  50.7 us
    all_to_all x1, waiting for transfers between devices, shards(): received = lax.all_to_all(jnp.stack(shards_2), 'cb', 0, 0)  37.5 us
    all_gather x1, waiting for transfers between devices, shards(): value_piece = lax.all_gather(projected[2], 'seq', axis=1, tiled=True)  24.7 us
    all_gather x1, waiting for transfers between devices, shards(): key_piece = lax.all_gather(projected[1], 'seq', axis=1, tiled=True)  21.2 us
    all_to_all x1, blocking collectives, shards(): lax.all_to_all(result, 'cb', split_axis=0, concat_axis=1, tiled=True)  17.5 us
    dot_general x3, matrix products, shards(): jnp.dot(normed, temporal_qkv[which], preferred_element_type=jnp.float32)  11.6 us
  transfers between devices with their start and end apart: 5, of which 5 were waited for; matrix products, arithmetic and copies ran while one was open for 7% of the time, Pallas kernels for 0%

profile of v1, /device:TPU:0, one launch (start us, length us, event | category | flops | bytes accessed | tf_op | source)
XLA Modules:
  0.0 333.7 jit_solution(13559045948277048717)
XLA Ops:
  12.3 3.5 %fusion.63 = bf16[256,512]{1,0:T(8,128)(2,1)S(1)} fusion(bf16[256,4096]{1,0:T(8,128)(2,1)S(1)} %bitcast.123, bf16[3,4096,512]{2,1,0:T(8,128)(2,1)} %param.12), kind=kOutput, calls=%fused_computation.55 | convolution fusion | flops 1073872896 | bytes 6553600 | tf_op jit(solution)/shard_map/dot_general | solution.py:37
  16.6 4.1 %fusion.57 = bf16[256,512]{1,0:T(8,128)(2,1)S(1)} fusion(bf16[256,4096]{1,0:T(8,128)(2,1)} %bitcast.124, bf16[3,4096,512]{2,1,0:T(8,128)(2,1)} %param.12), kind=kOutput, calls=%fused_computation.53 | convolution fusion | flops 1073872896 | bytes 6553600 | tf_op jit(solution)/shard_map/dot_general | solution.py:37
  21.7 4.1 %fusion.60 = bf16[256,512]{1,0:T(8,128)(2,1)S(1)} fusion(bf16[256,4096]{1,0:T(8,128)(2,1)} %bitcast.125, bf16[3,4096,512]{2,1,0:T(8,128)(2,1)} %param.12), kind=kOutput, calls=%fused_computation.54 | convolution fusion | flops 1073872896 | bytes 6553600 | tf_op jit(solution)/shard_map/dot_general | solution.py:37
  26.0 21.2 %all-gather.6.cloned.1.call-done = bf16[2,1024,4,128]{3,1,2,0:T(8,128)(2,1)} async-done(((bf16[2,128,4,128]{3,1,2,0:T(8,128)(2,1)}), bf16[2,1024,4,128]{3,1,2,0:T(8,128)(2,1)}) %all-gather.6.cloned.1.call-update) | async-done | bytes 2097168 | tf_op jit(solution)/shard_map/all_gather | solution.py:45
  47.3 2.6 fusion.12
  53.2 24.7 %all-gather.4.cloned.1.call-done = bf16[2,1024,4,128]{1,3,2,0:T(8,128)(2,1)} async-done(((bf16[2,128,4,128]{1,3,2,0:T(8,128)(2,1)}), bf16[2,1024,4,128]{1,3,2,0:T(8,128)(2,1)}) %all-gather.4.cloned.1.call-update) | async-done | bytes 2097168 | tf_op jit(solution)/shard_map/all_gather | solution.py:46
  77.8 4.2 %fusion.73 = bf16[2,128,4,128]{1,3,2,0:T(8,128)(2,1)S(1)} fusion(bf16[2,1024,4,128]{1,3,2,0:T(8,128)(2,1)} %all-gather.4.cloned.1.call-done, f32[2,4,128,1024]{3,2,1,0:T(8,128)} %copy-done.2, f32[2,4,128]{2,1,0:T(4,128)S(1)} %broadcast_maximum_fusion, pred[128,1024]{1,0:T(8,128)(4,1)S(1)} %iota_compare_fusion, f32[2,128,4]{1,2,0:T(4,128)S(1)} %bitcast.130), kind=kOutput, calls=%fused_computation.64 | convolution fusion | flops 273940480 | bytes 6692864 | tf_op jit(solution)/shard_map/shqk,skhd->sqhd/dot_general | solution.py:58
  82.3 4.8 %convolution_convert_fusion = bf16[256,4096]{1,0:T(8,128)(2,1)} fusion(bf16[512,4096]{1,0:T(8,128)(2,1)} %param.13, bf16[32,8,4,128]{3,2,1,0:T(4,128)(2,1)S(1)} %bitcast.128), kind=kOutput, calls=%fused_computation.3 | convolution fusion | flops 1074790400 | bytes 6553600 | tf_op jit(solution)/shard_map/dot_general | solution.py:71
  87.7 4.3 %gather_fusion = bf16[256,1024]{1,0:T(8,128)(2,1)S(1)} fusion(bf16[2048,1024]{1,0:T(8,128)(2,1)} %bitcast.121, s32[1024]{0:T(1024)S(1)} %pad_clamp_fusion), kind=kCustom, calls=%fused_computation | custom fusion | bytes 1049600 | tf_op jit(solution)/shard_map/jit(_take)/gather | solution.py:79
  92.0 81.3 %all-reduce.2.cloned.1.call-done = bf16[256,4096]{1,0:T(8,128)(2,1)} async-done(((bf16[256,4096]{1,0:T(8,128)(2,1)}), bf16[256,4096]{1,0:T(8,128)(2,1)}) %all-reduce.2.cloned.1.call-update) | async-done | bytes 2097168 | tf_op jit(solution)/shard_map/psum | solution.py:72
  173.3 4.3 %fusion.8 = bf16[256,4096]{1,0:T(8,128)(2,1)} fusion(bf16[256,4096]{1,0:T(8,128)(2,1)} %all-reduce.2.cloned.1.call-done, bf16[2,128,4096]{2,1,0:T(8,128)(2,1)} %param.10), kind=kLoop, calls=%fused_computation.11 | loop fusion | flops 4194304 | bytes 6291456 | tf_op jit(solution)/shard_map/convert_element_type | solution.py:73
  177.7 50.7 %all-gather.8.cloned.1.call-done = bf16[1,4096,1024]{2,1,0:T(8,128)(2,1)} async-done(((bf16[1,512,1024]{2,1,0:T(8,128)(2,1)}), bf16[1,4096,1024]{2,1,0:T(8,128)(2,1)}) %all-gather.8.cloned.1.call-update) | async-done | bytes 8388624 | tf_op jit(solution)/shard_map/all_gather | solution.py:76
  228.4 6.5 %fusion.66 = (f32[256]{0:T(256)S(1)}, bf16[256,1024]{1,0:T(8,128)(2,1)S(1)}) fusion(bf16[256,1024]{1,0:T(8,128)(2,1)S(1)} %gather_fusion, pred[256]{0:T(512)(128)(4,1)S(1)} %compare_and_fusion, bf16[256,4096]{1,0:T(8,128)(2,1)} %fusion.8, bf16[1,4096,1024]{2,1,0:T(8,128)(2,1)} %all-gather.8.cloned.1.call-done), kind=kOutput, calls=%fused_computation.56 | convolution fusion | flops 2149318400 | bytes 11535616 | tf_op jit(solution)/shard_map/dot_general | solution.py:74
  234.9 2.5 fusion.45
  237.4 2.4 fusion.48
  243.8 4.6 %all-to-all-start = ((bf16[4,1,1,64,3072]{4,3,2,1,0:T(8,128)(2,1)}), bf16[4,1,1,64,3072]{4,3,2,1,0:T(8,128)(2,1)}, u32[]{:S(2)}, u32[]{:S(2)}) async-start(bf16[4,1,1,64,3072]{4,3,2,1,0:T(8,128)(2,1)} %pad_maximum_fusion.1), calls=%async_computation | async-start | bytes 3145728 | tf_op jit(solution)/shard_map/all_to_all | solution.py:98
  248.4 37.5 %all-to-all-done = bf16[4,1,1,64,3072]{4,3,2,1,0:T(8,128)(2,1)} async-done(((bf16[4,1,1,64,3072]{4,3,2,1,0:T(8,128)(2,1)}), bf16[4,1,1,64,3072]{4,3,2,1,0:T(8,128)(2,1)}, u32[]{:S(2)}, u32[]{:S(2)}) %all-to-all-start) | async-done | bytes 1572896 | tf_op jit(solution)/shard_map/all_to_all | solution.py:98
  285.8 4.9 %reshape_reshape.3 = bf16[4,64,3,16,64]{4,3,2,1,0:T(8,128)(2,1)} reshape(bf16[4,1,1,64,3072]{4,3,2,1,0:T(8,128)(2,1)} %all-to-all-done) | data formatting | bytes 3145728 | tf_op jit(solution)/shard_map/reshape;reshape | solution.py:101
  290.7 3.5 %fusion.89 = (bf16[4,64,1,16,64]{4,3,2,1,0:T(8,128)(2,1)}, bf16[4,64,1,16,64]{4,3,2,1,0:T(8,128)(2,1)S(1)}, bf16[4,64,1,16,64]{4,3,2,1,0:T(8,128)(2,1)S(1)}) fusion(bf16[4,64,3,16,64]{4,3,2,1,0:T(8,128)(2,1)} %reshape_reshape.3), kind=kLoop, calls=%fused_computation.91 | loop fusion | bytes 3145728 | tf_op jit(solution)/shard_map/slice | solution.py:104
  294.2 2.9 fusion.69
  297.1 2.4 copy.60
  302.6 2.9 fusion.32
  307.1 17.5 %all_to_all.14 = bf16[4,1,64,1024]{3,2,1,0:T(8,128)(2,1)S(1)} all-to-all(bf16[4,1,64,1024]{3,2,1,0:T(8,128)(2,1)} %bitcast.126), channel_id=1, replica_groups=mesh['seq'=8,'cb'=4] {'cb'}, dimensions={0} | all-to-all | bytes 1048576 | tf_op jit(solution)/shard_map/all_to_all | solution.py:125
  324.6 2.5 fusion.42
  (50 shorter events, 19.9 us)
Async XLA Ops:
  7.2 317.4 %copy-start = (bf16[1,1024,1024]{2,1,0:T(8,128)(2,1)S(1)}, bf16[1,1024,1024]{2,1,0:T(8,128)(2,1)}, u32[]{:S(2)}) copy-start(bf16[1,1024,1024]{2,1,0:T(8,128)(2,1)} %param.19) | copy-start | bytes 6291460
  7.2 40.1 %all-gather.6.cloned.1.call-start = ((), (), s32[]{:S(2)}) async-start(), calls=%async_computation.3 | async-start | bytes 2359296 | tf_op jit(solution)/shard_map/all_gather | solution.py:45
  7.2 2.4 copy-start.1
  10.9 1.3 copy-start.3
  16.6 61.2 %all-gather.4.cloned.1.call-start = ((), (), s32[]{:S(2)}) async-start(), calls=%async_computation.2 | async-start | bytes 2359296 | tf_op jit(solution)/shard_map/all_gather | solution.py:46
  21.7 151.7 %all-reduce.2.cloned.1.call-start = ((), (), s32[]{:S(2)}) async-start(), calls=%async_computation.4 | async-start | bytes 4194304 | tf_op jit(solution)/shard_map/psum | solution.py:72
  49.9 1.9 copy-start.2
  87.0 0.7 copy-start.4
  87.0 141.4 %all-gather.8.cloned.1.call-start = ((), (), s32[]{:S(2)}) async-start(), calls=%async_computation.5 | async-start | bytes 9437184 | tf_op jit(solution)/shard_map/all_gather | solution.py:76
  177.7 57.2 %copy-start.5 = (f32[1,1024]{1,0:T(1,128)S(1)}, f32[1,1024]{1,0:T(1,128)}, u32[]{:S(2)}) copy-start(f32[1,1024]{1,0:T(1,128)} %param.17) | copy-start | bytes 12292
  234.9 4.9 %copy-start.6 = (bf16[256,1024]{1,0:T(8,128)(2,1)}, bf16[256,1024]{1,0:T(8,128)(2,1)S(1)}, u32[]{:S(2)}) copy-start(bf16[256,1024]{1,0:T(8,128)(2,1)S(1)} %get-tuple-element.24) | copy-start | bytes 1572868
  243.8 42.1 %all-to-all-start = ((bf16[4,1,1,64,3072]{4,3,2,1,0:T(8,128)(2,1)}), bf16[4,1,1,64,3072]{4,3,2,1,0:T(8,128)(2,1)}, u32[]{:S(2)}, u32[]{:S(2)}) async-start(bf16[4,1,1,64,3072]{4,3,2,1,0:T(8,128)(2,1)} %pad_maximum_fusion.1), calls=%async_computation | async-start | bytes 3145728 | tf_op jit(solution)/shard_map/all_to_all | solution.py:98
Sparse Core Ops, SparseCore 0:
  16.7 30.4 all-gather.5
  49.7 28.0 all-gather.3
  87.2 86.1 all-reduce.1
  175.1 53.2 all-gather.7
